TPU v7x, 512 devices: a whole 4x4x16 slice. The times are simulated.
512 devices in a mesh: img: 16 (over z_hi, y, core), term: 32 (over z_lo, x).
Axes of the slice: x: 4, y: 4, z: 16 (z_hi: 2, z_lo: 8; z = z_hi * 8 + z_lo), core: 2. Of those that a mesh axis runs over, the one named last changes fastest.
Arguments:
- patches: bfloat16 [64, 256, 1024], P('img', 'term'), may hold values from -6 to 6
- patch_mask: int32 [64, 256], P('img', 'term'), may hold values 0 or 1
- proj_weight: bfloat16 [1024, 30720], P('img', 'term'), may hold values from -0.1875 to 0.1875
- proj_bias: float32 [30720], P('term'), may hold values from -4 to 4
- slab: bfloat16 [8128, 30720], P('img', 'term'), may hold values from 0 to 2
- query_ids: int32 [1024, 32], replicated, may hold values from -1 to 30719, as said below
- term_weights: bfloat16 [1024, 32], replicated, may hold values from 0.25 to 4
Outputs:
- scores: float32 [1024, 8192], P('term', 'img')
Inputs may be any that keep to these rules, and one draw needn't show every extreme that they name: `query_ids`: within a query the non-negative ids are distinct and come before the padding slots; every query has at least 8 real terms and some query fills all 32 slots.
All inputs are finite; a program needn't handle non-finite values. No bound on the sum of `patch_mask` on one device may be relied on, other than what follows from the above.
Results may differ from a plain program's by a relative error of at most 0.0003.
Values may be sent and summed in bfloat16 or wider, within the bound.
A program may use at most 64 MiB of HBM per device.

v0:
```python
import jax
import jax.numpy as jnp
from jax import lax
from jax.sharding import PartitionSpec as P


def shards(patches, patch_mask, proj_weight, proj_bias, slab, query_ids, term_weights):
    proj_full = lax.all_gather(proj_weight, "img", axis=0, tiled=True)
    block_width = proj_full.shape[1]
    start_max = jnp.zeros((patches.shape[0], block_width), jnp.float32)
    features = lax.all_gather(patches, "term", axis=1, tiled=True)
    keep_mask = lax.all_gather(patch_mask.astype(jnp.bfloat16), "term", axis=1, tiled=True)
    logits = (
        jnp.einsum("npd,dv->npv", features, proj_full, preferred_element_type=jnp.float32)
        + proj_bias
    )
    activity = jnp.log1p(jnp.maximum(logits, 0.0))
    activity = jnp.where(keep_mask[:, :, None] > 0, activity, 0.0)
    pooled = jnp.maximum(start_max, jnp.max(activity, axis=1))
    impacts = jnp.concatenate([slab, pooled.astype(jnp.bfloat16)], axis=0)
    zero_value = jnp.zeros((), jnp.bfloat16)
    weights = jnp.where(query_ids >= 0, term_weights, zero_value)
    offset = lax.axis_index("term") * block_width
    columns = offset + lax.iota(jnp.int32, block_width)
    dense_rows = jnp.sum(
        jnp.where(query_ids[:, :, None] == columns[None, None, :], weights[:, :, None], zero_value),
        axis=1,
    )
    return lax.psum_scatter(
        lax.dot_general(
            dense_rows, impacts, (((1,), (1,)), ((), ())), preferred_element_type=jnp.float32
        ),
        "term",
        scatter_dimension=0,
        tiled=True,
    )


def solution(mesh):
    placed = (
        P("img", "term", None),
        P("img", "term"),
        P("img", "term"),
        P("term"),
        P("img", "term"),
        P(),
        P(),
    )
    return jax.shard_map(
        shards, mesh=mesh, in_specs=placed, out_specs=P("term", "img"), check_vma=False
    )
```

profile of v0, /device:TPU:24, one launch (start us, length us, event | category | flops | bytes accessed | tf_op | source)
XLA Modules:
  0.0 582.1 jit_solution(16606816592213149012)
XLA Ops:
  6.5 0.0 copy-start.1
  6.5 0.0 all-gather.6.cloned.1.call-start
  6.5 0.7 all-gather.6.cloned.1.call-update
  7.3 0.0 all-gather.4.cloned.1.call-start
  7.3 0.7 all-gather.4.cloned.1.call-update
  8.0 0.0 reduce-scatter.2.cloned.1.call-start
  8.1 0.7 convert_bitcast_fusion
  8.7 132.7 %all-gather = bf16[32,8,4]{1,2,0:T(4,128)(2,1)S(1)} all-gather(bf16[1,8,4]{1,2,0:T(4,128)(2,1)S(1)} %convert_bitcast_fusion), channel_id=1, replica_groups=mesh['img'=16,'term'=32] {'term'}, dimensions={0}, use_global_device_ids=true | all-gather | bytes 2112 | tf_op jit(solution)/shard_map/all_gather | solution.py:12
  141.4 0.1 copy.23
  141.5 0.1 copy.24
  141.6 0.1 reshape.12
  141.7 1.0 compare_select_fusion.1
  142.7 17.3 %fusion = bf16[1024,960]{0,1:T(8,128)(2,1)S(1)} fusion(s32[1024,32]{0,1:T(8,128)} %param.12, s32[960]{0:T(1024)S(1)} %iota_add_fusion, bf16[1024,32]{0,1:T(8,128)(2,1)S(1)} %compare_select_fusion.1), kind=kLoop, calls=%fused_computation.1 | loop fusion | flops 93388800 | bytes 2166528 | tf_op jit(solution)/shard_map/reduce_sum | solution.py:25
  160.1 0.0 all-gather.6.cloned.1.call-done
  160.1 163.3 %all-gather.4.cloned.1.call-done = bf16[4,256,1024]{2,1,0:T(8,128)(2,1)} async-done(((bf16[4,8,1024]{2,1,0:T(8,128)(2,1)}), bf16[4,256,1024]{2,1,0:T(8,128)(2,1)}) %all-gather.4.cloned.1.call-update) | async-done | bytes 2097168 | tf_op jit(solution)/shard_map/all_gather | solution.py:11
  323.4 0.0 copy-done.1
  323.4 0.0 copy-start
  323.4 6.1 %select_reduce_fusion = bf16[4,960]{1,0:T(4,128)(2,1)S(1)} fusion(f32[960]{0:T(1024)S(1)} %copy-done.1, pred[4,256]{1,0:T(4,128)(4,1)S(1)} %bitcast.14, bf16[4,256,1024]{2,1,0:T(8,128)(2,1)} %all-gather.4.cloned.1.call-done, bf16[1024,960]{1,0:T(8,128)(2,1)} %all-gather.6.cloned.1.call-done), kind=kOutput, calls=%fused_computation.2 | convolution fusion | flops 2017194240 | bytes 4075776 | tf_op jit(solution)/shard_map/npd,dv->npv/dot_general | solution.py:14
  329.5 0.2 copy.25
  329.7 0.0 copy-done
  329.8 2.7 fusion.5
  332.4 0.0 reduce-scatter.2.cloned.1.call-update
  332.5 243.2 %reduce-scatter.2.cloned.1.call-done = f32[32,512]{1,0:T(8,128)} async-done(((f32[1024,512]{1,0:T(8,128)}), f32[32,512]{1,0:T(8,128)}) %reduce-scatter.2.cloned.1.call-update) | async-done | bytes 65552 | tf_op jit(solution)/shard_map/reduce_scatter | solution.py:29
  (3 shorter events, 0.0 us)
Async XLA Ops:
  6.5 316.8 %copy-start.1 = (f32[960]{0:T(1024)S(1)}, f32[960]{0:T(1024)}, u32[]{:S(2)}) copy-start(f32[960]{0:T(1024)} %param.10) | copy-start | bytes 11524
  6.5 153.5 %all-gather.6.cloned.1.call-start = ((), (), s32[]{:S(2)}) async-start(), calls=%async_computation.2 | async-start | bytes 2228224 | tf_op jit(solution)/shard_map/all_gather | solution.py:8
  7.3 316.1 %all-gather.4.cloned.1.call-start = ((), (), s32[]{:S(2)}) async-start(), calls=%async_computation.1 | async-start | bytes 2162688 | tf_op jit(solution)/shard_map/all_gather | solution.py:11
  8.0 567.6 %reduce-scatter.2.cloned.1.call-start = ((), (), s32[]{:S(2)}) async-start(), calls=%async_computation.3 | async-start | bytes 2162688 | tf_op jit(solution)/shard_map/reduce_scatter | solution.py:29
  323.4 6.4 %copy-start = (bf16[508,960]{0,1:T(8,128)(2,1)S(1)}, bf16[508,960]{0,1:T(8,128)(2,1)}, u32[]{:S(2)}) copy-start(bf16[508,960]{0,1:T(8,128)(2,1)} %param.11) | copy-start | bytes 2926084
Sparse Core Ops, SparseCore 0:
  10.6 95.9 all-gather.5
  108.7 214.5 all-gather.3
  332.6 242.9 reduce-scatter.1
where the time goes:
time: 582 us
  waiting for transfers between devices  408 us (70%)
  blocking collectives  133 us (23%)
  other arithmetic  19 us (3%)
  between operations  13.2 us (2%)
  matrix products  8.82 us (2%)
    reduce_scatter x1, waiting for transfers between devices, shards(): lax.psum_scatter(lax.dot_general(dense_rows, impacts, (((1,), (1,)), ((),...  243 us
    all_gather x1, waiting for transfers between devices, shards(): features = lax.all_gather(patches, 'term', axis=1, tiled=True)  163 us
    all_gather x1, blocking collectives, shards(): lax.all_gather(patch_mask.astype(jnp.bfloat16), 'term', axis=1, tiled=True)  133 us
    reduce_sum x1, other arithmetic, shards(): jnp.sum(jnp.where(query_ids[:, :, None] == columns[None, None, :], weight...  17.3 us
  transfers between devices with their start and end apart: 3, of which 2 were waited for; matrix products, arithmetic and copies ran while one was open for 3% of the time, Pallas kernels for 0%

commit v1 on v0

--- a/solution.py
+++ b/solution.py
@@ -5,10 +5,18 @@
 
 
 def shards(patches, patch_mask, proj_weight, proj_bias, slab, query_ids, term_weights):
+
+    def things_update(a0):
+        res = lax.axis_size("term")
+        formed = lax.all_to_all(
+            jnp.stack(res * [a0]), axis_name="term", concat_axis=0, split_axis=0
+        )
+        return jnp.concatenate(formed, axis=1)
+
     proj_full = lax.all_gather(proj_weight, "img", axis=0, tiled=True)
     block_width = proj_full.shape[1]
     start_max = jnp.zeros((patches.shape[0], block_width), jnp.float32)
-    features = lax.all_gather(patches, "term", axis=1, tiled=True)
+    features = things_update(patches)
     keep_mask = lax.all_gather(patch_mask.astype(jnp.bfloat16), "term", axis=1, tiled=True)
     logits = (
         jnp.einsum("npd,dv->npv", features, proj_full, preferred_element_type=jnp.float32)

time: 582 us -> 483 us (0.83)
  waiting for transfers between devices: 408 us -> 252 us
  blocking collectives: 133 us -> 172 us
  starting transfers between devices: 0.08 us -> 15.6 us
    all_gather x1 -> x0, waiting for transfers between devices: 163 us -> none  [shards(): features = lax.all_gather(patches, 'term', axis=1, tiled=True)]
    all_gather x1, blocking collectives: 133 us -> 172 us  [shards(): lax.all_gather(patch_mask.astype(jnp.bfloat16), 'term', axis=1, tiled=True)]
    all_to_all x0 -> x1, starting transfers between devices: none -> 15.5 us  [things_update(): lax.all_to_all(jnp.stack(res * [a0]), axis_name='term', concat_axis=0, sp...]
    reduce_scatter x1, waiting for transfers between devices: 243 us -> 251 us  [shards(): lax.psum_scatter(lax.dot_general(dense_rows, impacts, (((1,), (1,)), ((),...]
  transfers between devices with their start and end apart: 3 -> 3, of which waited for: 2 -> 1; matrix products, arithmetic and copies ran while one was open for 3% -> 4% of each run, Pallas kernels for 0% -> 0%
where the time goes in v1:
time: 483 us
  waiting for transfers between devices  252 us (52%)
  blocking collectives  172 us (36%)
  other arithmetic  17.4 us (4%)
  starting transfers between devices  15.6 us (3%)
  between operations  13.5 us (3%)
  matrix products  9.73 us (2%)
    reduce_scatter x1, waiting for transfers between devices, shards(): lax.psum_scatter(lax.dot_general(dense_rows, impacts, (((1,), (1,)), ((),...  251 us
    all_gather x1, blocking collectives, shards(): lax.all_gather(patch_mask.astype(jnp.bfloat16), 'term', axis=1, tiled=True)  172 us
    reduce_sum x1, other arithmetic, shards(): jnp.sum(jnp.where(query_ids[:, :, None] == columns[None, None, :], weight...  17.3 us
    all_to_all x1, starting transfers between devices, things_update(): lax.all_to_all(jnp.stack(res * [a0]), axis_name='term', concat_axis=0, sp...  15.5 us
  transfers between devices with their start and end apart: 3, of which 1 were waited for; matrix products, arithmetic and copies ran while one was open for 4% of the time, Pallas kernels for 0%

profile of v1, /device:TPU:24, one launch (start us, length us, event | category | flops | bytes accessed | tf_op | source)
XLA Modules:
  0.0 482.9 jit_solution(4892524763893936108)
XLA Ops:
  6.5 2.4 stack.2
  8.9 0.0 copy-start.2
  8.9 0.0 copy-start
  8.9 0.0 copy-start.1
  8.9 15.5 %all-to-all-start = ((bf16[32,4,8,1024]{3,2,1,0:T(8,128)(2,1)}), bf16[32,4,8,1024]{3,2,1,0:T(8,128)(2,1)S(1)}, u32[]{:S(2)}, u32[]{:S(2)}) async-start(bf16[32,4,8,1024]{3,2,1,0:T(8,128)(2,1)} %stack.2), calls=%async_computation | async-start | bytes 4194304 | tf_op jit(solution)/shard_map/all_to_all | solution.py:11
  24.5 0.0 copy-start.4
  24.5 0.0 all-gather.3.cloned.1.call-start
  24.5 0.7 all-gather.3.cloned.1.call-update
  25.2 0.0 reduce-scatter.2.cloned.1.call-start
  25.3 0.0 copy-done.2
  25.3 171.7 %all-gather = bf16[32,8,4]{1,2,0:T(4,128)(2,1)S(1)} all-gather(bf16[1,8,4]{1,2,0:T(4,128)(2,1)S(1)} %convert_bitcast_fusion), channel_id=1, replica_groups=mesh['img'=16,'term'=32] {'term'}, dimensions={0}, use_global_device_ids=true | all-gather | bytes 2112 | tf_op jit(solution)/shard_map/all_gather | solution.py:20
  197.0 0.1 copy.26
  197.1 0.1 copy.27
  197.2 0.1 reshape.22
  197.3 0.0 copy-done
  197.3 0.0 copy-done.1
  197.4 17.3 %fusion = bf16[1024,960]{0,1:T(8,128)(2,1)} fusion(s32[1024,32]{0,1:T(8,128)S(1)} %copy-done, s32[960]{0:T(1024)S(1)} %iota_add_fusion, bf16[1024,32]{0,1:T(8,128)(2,1)S(1)} %compare_select_fusion.1), kind=kLoop, calls=%fused_computation.1 | loop fusion | flops 93388800 | bytes 2166528 | tf_op jit(solution)/shard_map/reduce_sum | solution.py:33
  214.7 0.0 all-gather.3.cloned.1.call-done
  214.7 0.0 all-to-all-done
  214.7 0.0 copy-done.4
  214.7 0.0 copy-start.3
  214.7 5.5 %select_reduce_fusion = bf16[4,960]{1,0:T(4,128)(2,1)S(1)} fusion(f32[960]{0:T(1024)S(1)} %copy-done.4, pred[4,256]{1,0:T(4,128)(4,1)S(1)} %bitcast.20, bf16[1024,960]{1,0:T(8,128)(2,1)} %all-gather.3.cloned.1.call-done, bf16[32,4,8,1024]{3,2,1,0:T(8,128)(2,1)S(1)} %all-to-all-done), kind=kOutput, calls=%fused_computation.2 | convolution fusion | flops 2017194240 | bytes 4075776 | tf_op jit(solution)/shard_map/npd,dv->npv/dot_general | solution.py:22
  220.2 0.2 copy.29
  220.4 0.0 copy-done.3
  220.4 4.2 fusion.9
  224.7 0.0 reduce-scatter.2.cloned.1.call-update
  224.7 251.4 %reduce-scatter.2.cloned.1.call-done = f32[32,512]{1,0:T(8,128)} async-done(((f32[1024,512]{1,0:T(8,128)}), f32[32,512]{1,0:T(8,128)}) %reduce-scatter.2.cloned.1.call-update) | async-done | bytes 65552 | tf_op jit(solution)/shard_map/reduce_scatter | solution.py:37
  (5 shorter events, 0.0 us)
Async XLA Ops:
  8.9 16.3 %copy-start.2 = (s32[4,8]{1,0:T(4,128)S(1)}, s32[4,8]{1,0:T(4,128)}, u32[]{:S(2)}) copy-start(s32[4,8]{1,0:T(4,128)} %param.8) | copy-start | bytes 388
  8.9 188.4 %copy-start = (s32[1024,32]{0,1:T(8,128)S(1)}, s32[1024,32]{0,1:T(8,128)}, u32[]{:S(2)}) copy-start(s32[1024,32]{0,1:T(8,128)} %param.12) | copy-start | bytes 393220
  8.9 188.4 %copy-start.1 = (bf16[1024,32]{0,1:T(8,128)(2,1)S(1)}, bf16[1024,32]{0,1:T(8,128)(2,1)}, u32[]{:S(2)}) copy-start(bf16[1024,32]{0,1:T(8,128)(2,1)} %param.13) | copy-start | bytes 196612
  8.9 205.7 %all-to-all-start = ((bf16[32,4,8,1024]{3,2,1,0:T(8,128)(2,1)}), bf16[32,4,8,1024]{3,2,1,0:T(8,128)(2,1)S(1)}, u32[]{:S(2)}, u32[]{:S(2)}) async-start(bf16[32,4,8,1024]{3,2,1,0:T(8,128)(2,1)} %stack.2), calls=%async_computation | async-start | bytes 4194304 | tf_op jit(solution)/shard_map/all_to_all | solution.py:11
  24.5 190.2 %copy-start.4 = (f32[960]{0:T(1024)S(1)}, f32[960]{0:T(1024)}, u32[]{:S(2)}) copy-start(f32[960]{0:T(1024)} %param.10) | copy-start | bytes 11524
  24.5 190.2 %all-gather.3.cloned.1.call-start = ((), (), s32[]{:S(2)}) async-start(), calls=%async_computation.2 | async-start | bytes 2228224 | tf_op jit(solution)/shard_map/all_gather | solution.py:16
  25.2 450.9 %reduce-scatter.2.cloned.1.call-start = ((), (), s32[]{:S(2)}) async-start(), calls=%async_computation.3 | async-start | bytes 2162688 | tf_op jit(solution)/shard_map/reduce_scatter | solution.py:37
  214.7 5.7 %copy-start.3 = (bf16[508,960]{0,1:T(8,128)(2,1)S(1)}, bf16[508,960]{0,1:T(8,128)(2,1)}, u32[]{:S(2)}) copy-start(bf16[508,960]{0,1:T(8,128)(2,1)} %param.11) | copy-start | bytes 2926084
Sparse Core Ops, SparseCore 0:
  28.6 98.7 all-gather.2
  224.8 251.2 reduce-scatter.1
